TPU v7x, 32 devices: a whole 2x2x4 slice. The times are simulated.
32 devices in a mesh: dp: 4 (over x, core), tensor: 8 (over z, y).
Axes of the slice: x: 2, y: 2, z: 4, core: 2. Of those that a mesh axis runs over, the one named last changes fastest.
Arguments:
- hidden: bfloat16 [3072, 4096], P('dp', 'tensor'), may hold values from -2000 to 2000
- out_embed: bfloat16 [16384, 4096], P('tensor', 'dp'), may hold values from -0.3 to 0.3
- labels: int32 [3072], P('dp'), may hold values from 0 to 16383
Outputs:
- token_loss: float32 [3072], P(('dp', 'tensor'))
- mean_loss: float32 [], replicated
All inputs are finite; a program needn't handle non-finite values.
Results may differ from a plain program's by a relative error of at most 0.0003.
Values may be sent and summed in bfloat16 or wider, within the bound.
No kernel may reach another device: no remote copies, remote signals or barrier semaphores. Data moves between devices by JAX's collectives and lax.ppermute only.
A program may use at most 128 MiB of HBM per device.

v0:
```python
import jax
import jax.numpy as jnp
from jax import lax
from jax.sharding import PartitionSpec as P

BLOCK = 512


def combine_stats(first, second):
    peak_first, mass_first, label_first = first
    peak_second, mass_second, label_second = second
    peak_value = jnp.maximum(peak_first, peak_second)
    exp_total = mass_first * jnp.exp(peak_first - peak_value) + mass_second * jnp.exp(
        peak_second - peak_value
    )
    return (peak_value, exp_total, label_first + label_second)


def block_stats(logits, first_row, labels):
    peak_value = jnp.max(logits, axis=0)
    exp_total = jnp.sum(jnp.exp(logits - peak_value[None, :]), axis=0)
    row_ids = first_row + lax.broadcasted_iota(jnp.int32, logits.shape, 0)
    label_logit = jnp.sum(
        jnp.where(row_ids == labels[None, :], logits, jnp.zeros_like(logits)), axis=0
    )
    return (peak_value, exp_total, label_logit)


def body(hidden, out_embed, labels):
    full_hidden = lax.all_gather(hidden, "tensor", axis=1, tiled=True)
    token_count = full_hidden.shape[0]
    vocab_rows = out_embed.shape[0]
    vocab_offset = lax.axis_index("tensor") * vocab_rows
    block_count = vocab_rows // BLOCK
    running_stats = None
    for block_index in range(block_count):
        weight_block = out_embed[block_index * BLOCK : (block_index + 1) * BLOCK]
        stats = block_stats(
            lax.dot_general(
                lax.all_gather(weight_block, "dp", axis=1, tiled=True),
                full_hidden,
                (((1,), (1,)), ((), ())),
                preferred_element_type=jnp.float32,
            ),
            vocab_offset + block_index * BLOCK,
            labels,
        )
        running_stats = stats if running_stats is None else combine_stats(running_stats, stats)
    groups = lax.axis_size("tensor")
    share = token_count // groups
    peak_all, mass_all, label_all = running_stats
    peaks, masses, picked = (
        lax.all_to_all(
            peak_all.reshape(groups, share), "tensor", split_axis=0, concat_axis=0, tiled=True
        ),
        lax.all_to_all(
            mass_all.reshape(groups, share), "tensor", split_axis=0, concat_axis=0, tiled=True
        ),
        lax.all_to_all(
            label_all.reshape(groups, share), "tensor", split_axis=0, concat_axis=0, tiled=True
        ),
    )
    peak_value = jnp.max(peaks, axis=0)
    exp_total = jnp.sum(masses * jnp.exp(peaks - peak_value[None, :]), axis=0)
    label_logit = jnp.sum(picked, axis=0)
    token_loss = jnp.log(exp_total) + peak_value - label_logit
    loss_sum = lax.psum(jnp.sum(token_loss), ("dp", "tensor"))
    mean_loss = loss_sum / (share * lax.axis_size("dp") * groups)
    return (token_loss, mean_loss)


def solution(mesh):
    return jax.shard_map(
        body,
        mesh=mesh,
        in_specs=(P("dp", "tensor"), P("tensor", "dp"), P("dp")),
        out_specs=(P(("dp", "tensor")), P()),
        check_vma=False,
    )
```

profile of v0, /device:TPU:0, one launch (start us, length us, event | category | flops | bytes accessed | tf_op | source)
XLA Modules:
  0.0 347.8 jit_solution(11114172861355873410)
XLA Ops:
  7.2 4.2 %fusion.2 = (bf16[512,1024]{1,0:T(8,128)(2,1)}, bf16[512,1024]{1,0:T(8,128)(2,1)}, bf16[512,1024]{1,0:T(8,128)(2,1)}, bf16[512,1024]{1,0:T(8,128)(2,1)}) fusion(bf16[2048,1024]{1,0:T(8,128)(2,1)} %param.4), kind=kLoop, calls=%fused_computation.18 | loop fusion | bytes 8388608 | tf_op jit(solution)/shard_map/slice | solution.py:37
  11.5 0.7 all-gather.8.cloned.1.call-update
  12.3 0.7 all-gather.10.cloned.1.call-update
  13.0 0.5 all-gather.12.cloned.1.call-update
  13.6 0.5 all-gather.14.cloned.1.call-update
  14.2 34.7 %all-gather.6.cloned.1.call-done = bf16[512,4096]{1,0:T(8,128)(2,1)} async-done(((bf16[512,1024]{1,0:T(8,128)(2,1)}), bf16[512,4096]{1,0:T(8,128)(2,1)}) %all-gather.6.cloned.1.call-update) | async-done | bytes 4194320 | tf_op jit(solution)/shard_map/all_gather | solution.py:40
  48.8 101.6 %all-gather.8.cloned.1.call-done = bf16[768,4096]{1,0:T(8,128)(2,1)} async-done(((bf16[768,512]{1,0:T(8,128)(2,1)}), bf16[768,4096]{1,0:T(8,128)(2,1)}) %all-gather.8.cloned.1.call-update) | async-done | bytes 6291472 | tf_op jit(solution)/shard_map/all_gather | solution.py:30
  150.4 7.1 %fusion.6 = (f32[768]{0:T(1024)S(1)}, f32[512,768]{1,0:T(8,128)S(1)}) fusion(bf16[512,4096]{1,0:T(8,128)(2,1)} %all-gather.6.cloned.1.call-done, bf16[768,4096]{1,0:T(8,128)(2,1)} %all-gather.8.cloned.1.call-done), kind=kOutput, calls=%fused_computation.22 | convolution fusion | flops 3221617920 | bytes 12061696 | tf_op jit(solution)/shard_map/dot_general | solution.py:39
  157.5 0.1 reduce_max.54
  157.6 27.0 %all-gather.10.cloned.1.call-done = bf16[512,4096]{1,0:T(8,128)(2,1)} async-done(((bf16[512,1024]{1,0:T(8,128)(2,1)}), bf16[512,4096]{1,0:T(8,128)(2,1)}) %all-gather.10.cloned.1.call-update) | async-done | bytes 4194320 | tf_op jit(solution)/shard_map/all_gather | solution.py:40
  184.6 7.1 %fusion.3 = (f32[768]{0:T(1024)S(1)}, f32[512,768]{1,0:T(8,128)S(1)}) fusion(bf16[512,4096]{1,0:T(8,128)(2,1)} %all-gather.10.cloned.1.call-done, bf16[768,4096]{1,0:T(8,128)(2,1)} %all-gather.8.cloned.1.call-done), kind=kOutput, calls=%fused_computation.19 | convolution fusion | flops 3221617920 | bytes 12061696 | tf_op jit(solution)/shard_map/dot_general | solution.py:39
  191.7 0.1 reduce_max.56
  191.8 28.7 %all-gather.12.cloned.1.call-done = bf16[512,4096]{1,0:T(8,128)(2,1)} async-done(((bf16[512,1024]{1,0:T(8,128)(2,1)}), bf16[512,4096]{1,0:T(8,128)(2,1)}) %all-gather.12.cloned.1.call-update) | async-done | bytes 4194320 | tf_op jit(solution)/shard_map/all_gather | solution.py:40
  220.5 8.7 %fusion.4 = (f32[768]{0:T(1024)S(1)}, f32[512,768]{1,0:T(8,128)}) fusion(bf16[512,4096]{1,0:T(8,128)(2,1)} %all-gather.12.cloned.1.call-done, bf16[768,4096]{1,0:T(8,128)(2,1)} %all-gather.8.cloned.1.call-done), kind=kOutput, calls=%fused_computation.20 | convolution fusion | flops 3221617920 | bytes 12061696 | tf_op jit(solution)/shard_map/dot_general | solution.py:39
  229.2 0.1 reduce_max.58
  229.3 27.1 %all-gather.14.cloned.1.call-done = bf16[512,4096]{1,0:T(8,128)(2,1)} async-done(((bf16[512,1024]{1,0:T(8,128)(2,1)}), bf16[512,4096]{1,0:T(8,128)(2,1)}) %all-gather.14.cloned.1.call-update) | async-done | bytes 4194320 | tf_op jit(solution)/shard_map/all_gather | solution.py:40
  256.4 8.7 %fusion.5 = (f32[768]{0:T(1024)S(1)}, f32[512,768]{1,0:T(8,128)}) fusion(bf16[512,4096]{1,0:T(8,128)(2,1)} %all-gather.14.cloned.1.call-done, bf16[768,4096]{1,0:T(8,128)(2,1)} %all-gather.8.cloned.1.call-done), kind=kOutput, calls=%fused_computation.21 | convolution fusion | flops 3221617920 | bytes 12061696 | tf_op jit(solution)/shard_map/dot_general | solution.py:39
  265.1 0.1 reduce_max.60
  265.1 3.2 exponential_reduce_fusion.2
  268.4 0.1 reduce_sum.108
  268.4 0.1 reduce_sum.110
  268.5 0.1 reduce_sum.112
  268.6 0.1 reduce_sum.114
  268.7 0.6 multiply_add_fusion
  269.3 5.5 %all-to-all-start.1 = ((f32[8,1,96]{2,1,0:T(1,128)}), f32[8,1,96]{2,1,0:T(1,128)S(1)}, u32[]{:S(2)}, u32[]{:S(2)}) async-start(f32[8,1,96]{2,1,0:T(1,128)} %bitcast.2), calls=%async_computation.1 | async-start | bytes 8192 | tf_op jit(solution)/shard_map/all_to_all | solution.py:53
  274.8 0.1 add.131
  274.9 6.4 %all-to-all-done.1 = f32[8,1,96]{2,1,0:T(1,128)S(1)} async-done(((f32[8,1,96]{2,1,0:T(1,128)}), f32[8,1,96]{2,1,0:T(1,128)S(1)}, u32[]{:S(2)}, u32[]{:S(2)}) %all-to-all-start.1) | async-done | bytes 3104 | tf_op jit(solution)/shard_map/all_to_all | solution.py:53
  281.3 8.8 %all_to_all.24 = f32[8,1,96]{2,1,0:T(1,128)S(1)} all-to-all(f32[8,1,96]{2,1,0:T(1,128)S(1)} %add.131), channel_id=1, replica_groups=mesh['dp'=4,'tensor'=8] {'tensor'}, dimensions={0} | all-to-all | bytes 6144 | tf_op jit(solution)/shard_map/all_to_all | solution.py:59
  290.1 3.3 all-to-all-start
  293.5 6.4 %all-to-all-done = f32[8,1,96]{2,1,0:T(1,128)S(1)} async-done(((f32[8,1,96]{2,1,0:T(1,128)}), f32[8,1,96]{2,1,0:T(1,128)S(1)}, u32[]{:S(2)}, u32[]{:S(2)}) %all-to-all-start) | async-done | bytes 3104 | tf_op jit(solution)/shard_map/all_to_all | solution.py:56
  299.9 1.1 fusion
  301.0 38.4 %psum.7 = f32[]{:T(128)} all-reduce(f32[]{:T(128)} %get-tuple-element.10), channel_id=1, replica_groups=mesh['dp'=4,'tensor'=8] {'dp','tensor'}, use_global_device_ids=true, to_apply=%region_16.17 | all-reduce | flops 1 | bytes 8 | tf_op jit(solution)/shard_map/psum | solution.py:67
  (15 shorter events, 0.3 us)
Async XLA Ops:
  7.2 41.6 %all-gather.6.cloned.1.call-start = ((), (), s32[]{:S(2)}) async-start(), calls=%async_computation.3 | async-start | bytes 5242880 | tf_op jit(solution)/shard_map/all_gather | solution.py:40
  11.5 138.9 %all-gather.8.cloned.1.call-start = ((), (), s32[]{:S(2)}) async-start(), calls=%async_computation.4 | async-start | bytes 7077888 | tf_op jit(solution)/shard_map/all_gather | solution.py:30
  12.2 172.4 %all-gather.10.cloned.1.call-start = ((), (), s32[]{:S(2)}) async-start(), calls=%async_computation.5 | async-start | bytes 5242880 | tf_op jit(solution)/shard_map/all_gather | solution.py:40
  13.0 207.5 %all-gather.12.cloned.1.call-start = ((), (), s32[]{:S(2)}) async-start(), calls=%async_computation.6 | async-start | bytes 5242880 | tf_op jit(solution)/shard_map/all_gather | solution.py:40
  13.5 242.9 %all-gather.14.cloned.1.call-start = ((), (), s32[]{:S(2)}) async-start(), calls=%async_computation.7 | async-start | bytes 5242880 | tf_op jit(solution)/shard_map/all_gather | solution.py:40
  229.3 35.9 %copy-start = (s32[768]{0:T(1024)S(1)}, s32[768]{0:T(1024)}, u32[]{:S(2)}) copy-start(s32[768]{0:T(1024)} %param.5) | copy-start | bytes 9220
  269.3 12.0 %all-to-all-start.1 = ((f32[8,1,96]{2,1,0:T(1,128)}), f32[8,1,96]{2,1,0:T(1,128)S(1)}, u32[]{:S(2)}, u32[]{:S(2)}) async-start(f32[8,1,96]{2,1,0:T(1,128)} %bitcast.2), calls=%async_computation.1 | async-start | bytes 8192 | tf_op jit(solution)/shard_map/all_to_all | solution.py:53
  290.1 9.8 %all-to-all-start = ((f32[8,1,96]{2,1,0:T(1,128)}), f32[8,1,96]{2,1,0:T(1,128)S(1)}, u32[]{:S(2)}, u32[]{:S(2)}) async-start(f32[8,1,96]{2,1,0:T(1,128)} %bitcast), calls=%async_computation | async-start | bytes 8192 | tf_op jit(solution)/shard_map/all_to_all | solution.py:56
Sparse Core Ops, SparseCore 0:
  11.6 37.1 all-gather.5
  50.9 99.4 all-gather.7
  151.9 32.6 all-gather.9
  186.0 34.4 all-gather.11
  221.9 34.4 all-gather.13
where the time goes:
time: 348 us
  waiting for transfers between devices  234 us (67%)
  blocking collectives  47.2 us (14%)
  matrix products  31.6 us (9%)
  between operations  15.6 us (4%)
  starting transfers between devices  9.04 us (3%)
  other arithmetic  5.05 us (1%)
  local copies, waits for them, and re-layouts  4.9 us (1%)
    all_gather x4, waiting for transfers between devices, body(): lax.all_gather(weight_block, 'dp', axis=1, tiled=True)  118 us
    all_gather x1, waiting for transfers between devices, body(): full_hidden = lax.all_gather(hidden, 'tensor', axis=1, tiled=True)  102 us
    psum x1, blocking collectives, body(): loss_sum = lax.psum(jnp.sum(token_loss), ('dp', 'tensor'))  38.4 us
    dot_general x4, matrix products, body(): lax.dot_general(lax.all_gather(weight_block, 'dp', axis=1, tiled=True), f...  31.6 us
    all_to_all x1, blocking collectives, body(): lax.all_to_all(label_all.reshape(groups, share), 'tensor', split_axis=0,...  8.85 us
  transfers between devices with their start and end apart: 7, of which 7 were waited for; matrix products, arithmetic and copies ran while one was open for 7% of the time, Pallas kernels for 0%

commit v1 on v0

--- a/solution.py
+++ b/solution.py
@@ -35,9 +35,24 @@
     running_stats = None
     for block_index in range(block_count):
         weight_block = out_embed[block_index * BLOCK : (block_index + 1) * BLOCK]
+
+        def _get_map(local, net_axis):
+            earlier = lax.axis_size(net_axis)
+            out_arr, outcome_arr = (earlier, lax.axis_index(net_axis))
+            m_next, item_now = (local, 1)
+            while item_now < out_arr:
+                local_now = lax.ppermute(
+                    m_next, axis_name=net_axis, perm=[(j0, j0 ^ item_now) for j0 in range(out_arr)]
+                )
+                y2 = jnp.concatenate([m_next, local_now], axis=1)
+                all_values = jnp.concatenate([local_now, m_next], axis=1)
+                m_next = jnp.where(outcome_arr & item_now == 0, y2, all_values)
+                item_now = 2 * item_now
+            return m_next
+
         stats = block_stats(
             lax.dot_general(
-                lax.all_gather(weight_block, "dp", axis=1, tiled=True),
+                _get_map(weight_block, "dp"),
                 full_hidden,
                 (((1,), (1,)), ((), ())),
                 preferred_element_type=jnp.float32,

time: 348 us -> 306 us (0.88)
  waiting for transfers between devices: 234 us -> 165 us
  other arithmetic: 5.05 us -> 19.3 us
  matrix products: 31.6 us -> 38.8 us
  starting transfers between devices: 9.04 us -> 15.4 us
    all_gather x4 -> x0, waiting for transfers between devices: 118 us -> none  [body(): lax.all_gather(weight_block, 'dp', axis=1, tiled=True)]
    ppermute x0 -> x8, waiting for transfers between devices: none -> 108 us  [_get_map(): lax.ppermute(m_next, axis_name=net_axis, perm=[(j0, j0 ^ item_now) for j0...]
    all_gather x1, waiting for transfers between devices: 102 us -> 43.3 us  [body(): full_hidden = lax.all_gather(hidden, 'tensor', axis=1, tiled=True)]
    select_n x0 -> x4, other arithmetic: none -> 14.3 us  [_get_map(): m_next = jnp.where(outcome_arr & item_now == 0, y2, all_values)]
    dot_general x4, matrix products: 31.6 us -> 38.8 us  [body(): lax.dot_general(_get_map(weight_block, 'dp'), full_hidden, (((1,), (1,)),...]
    ppermute x0 -> x8, starting transfers between devices: none -> 5.96 us  [_get_map(): lax.ppermute(m_next, axis_name=net_axis, perm=[(j0, j0 ^ item_now) for j0...]
  transfers between devices with their start and end apart: 7 -> 11, of which waited for: 7 -> 6; matrix products, arithmetic and copies ran while one was open for 7% -> 15% of each run, Pallas kernels for 0% -> 0%
where the time goes in v1:
time: 306 us
  waiting for transfers between devices  165 us (54%)
  blocking collectives  47.3 us (15%)
  matrix products  38.8 us (13%)
  other arithmetic  19.3 us (6%)
  between operations  15.9 us (5%)
  starting transfers between devices  15.4 us (5%)
  local copies, waits for them, and re-layouts  4.52 us (1%)
    ppermute x8, waiting for transfers between devices, _get_map(): lax.ppermute(m_next, axis_name=net_axis, perm=[(j0, j0 ^ item_now) for j0...  108 us
    all_gather x1, waiting for transfers between devices, body(): full_hidden = lax.all_gather(hidden, 'tensor', axis=1, tiled=True)  43.3 us
    dot_general x4, matrix products, body(): lax.dot_general(_get_map(weight_block, 'dp'), full_hidden, (((1,), (1,)),...  38.8 us
    psum x1, blocking collectives, body(): loss_sum = lax.psum(jnp.sum(token_loss), ('dp', 'tensor'))  38.5 us
    select_n x4, other arithmetic, _get_map(): m_next = jnp.where(outcome_arr & item_now == 0, y2, all_values)  14.3 us
    all_to_all x1, blocking collectives, body(): lax.all_to_all(label_all.reshape(groups, share), 'tensor', split_axis=0,...  8.85 us
    all_to_all x1, waiting for transfers between devices, body(): lax.all_to_all(peak_all.reshape(groups, share), 'tensor', split_axis=0, c...  6.4 us
    all_to_all x1, waiting for transfers between devices, body(): lax.all_to_all(mass_all.reshape(groups, share), 'tensor', split_axis=0, c...  6.38 us
  transfers between devices with their start and end apart: 11, of which 6 were waited for; matrix products, arithmetic and copies ran while one was open for 15% of the time, Pallas kernels for 0%

profile of v1, /device:TPU:0, one launch (start us, length us, event | category | flops | bytes accessed | tf_op | source)
XLA Modules:
  0.0 305.8 jit_solution(17577606705843589255)
XLA Ops:
  7.2 0.7 all-gather.2.cloned.1.call-update
  7.9 3.9 %fusion.34 = (bf16[512,1024]{1,0:T(8,128)(2,1)S(1)}, bf16[512,1024]{1,0:T(8,128)(2,1)}, bf16[512,1024]{1,0:T(8,128)(2,1)S(1)}, bf16[512,1024]{1,0:T(8,128)(2,1)S(1)}) fusion(bf16[2048,1024]{1,0:T(8,128)(2,1)} %param.4), kind=kLoop, calls=%fused_computation.58 | loop fusion | bytes 8388608 | tf_op jit(solution)/shard_map/slice | solution.py:37
  11.8 0.5 collective-permute-start
  12.3 2.6 collective-permute-done
  14.9 4.4 %maximum_select_fusion.8 = bf16[512,2048]{1,0:T(8,128)(2,1)} fusion(bf16[512,1024]{1,0:T(8,128)(2,1)} %collective-permute-done, bf16[512,1024]{1,0:T(8,128)(2,1)} %get-tuple-element.17, pred[]{:T(512)S(6)} %eq.15), kind=kLoop, calls=%fused_computation.32 | loop fusion | flops 9437184 | bytes 4194305 | tf_op jit(solution)/shard_map/jit(_where)/select_n | solution.py:49
  19.3 2.8 collective-permute-start.1
  22.2 0.5 collective-permute-start.2
  22.7 3.8 %maximum_select_fusion.10 = bf16[512,2048]{1,0:T(8,128)(2,1)} fusion(bf16[512,1024]{1,0:T(8,128)(2,1)} %collective-permute-done.4, bf16[512,1024]{1,0:T(8,128)(2,1)S(1)} %get-tuple-element.19, pred[]{:T(512)S(6)} %eq.15), kind=kLoop, calls=%fused_computation.34 | loop fusion | flops 9437184 | bytes 4194305 | tf_op jit(solution)/shard_map/jit(_where)/select_n | solution.py:49
  26.5 3.7 %maximum_select_fusion.11 = bf16[512,2048]{1,0:T(8,128)(2,1)} fusion(bf16[512,1024]{1,0:T(8,128)(2,1)} %collective-permute-done.6, bf16[512,1024]{1,0:T(8,128)(2,1)S(1)} %get-tuple-element.18, pred[]{:T(512)S(6)} %eq.15), kind=kLoop, calls=%fused_computation.35 | loop fusion | flops 9437184 | bytes 4194305 | tf_op jit(solution)/shard_map/jit(_where)/select_n | solution.py:49
  30.2 2.0 collective-permute-start.7
  32.2 2.3 maximum_select_fusion.9
  34.6 0.1 collective-permute-start.3
  34.7 34.3 %collective-permute-done.1 = bf16[512,2048]{1,0:T(8,128)(2,1)} collective-permute-done((bf16[512,2048]{1,0:T(8,128)(2,1)}, bf16[512,2048]{1,0:T(8,128)(2,1)}, u32[]{:S(2)}, u32[]{:S(2)}) %collective-permute-start.1) | collective-permute-done | bytes 2097184 | tf_op jit(solution)/shard_map/ppermute | solution.py:44
  69.0 43.3 %all-gather.2.cloned.1.call-done = bf16[768,4096]{1,0:T(8,128)(2,1)} async-done(((bf16[768,512]{1,0:T(8,128)(2,1)}), bf16[768,4096]{1,0:T(8,128)(2,1)}) %all-gather.2.cloned.1.call-update) | async-done | bytes 6291472 | tf_op jit(solution)/shard_map/all_gather | solution.py:30
  112.3 9.9 %fusion.38 = (f32[768]{0:T(1024)S(1)}, f32[512,768]{1,0:T(8,128)}) fusion(bf16[768,4096]{1,0:T(8,128)(2,1)} %all-gather.2.cloned.1.call-done, bf16[512,2048]{1,0:T(8,128)(2,1)} %collective-permute-done.1, bf16[512,2048]{1,0:T(8,128)(2,1)} %maximum_select_fusion.8, pred[]{:T(512)S(6)} %eq.14), kind=kOutput, calls=%fused_computation.62 | convolution fusion | flops 3240492288 | bytes 12061697 | tf_op jit(solution)/shard_map/dot_general | solution.py:54
  122.2 10.0 %fusion.36 = (f32[768]{0:T(1024)S(1)}, f32[512,768]{1,0:T(8,128)}) fusion(bf16[768,4096]{1,0:T(8,128)(2,1)} %all-gather.2.cloned.1.call-done, bf16[512,2048]{1,0:T(8,128)(2,1)} %collective-permute-done.5, bf16[512,2048]{1,0:T(8,128)(2,1)} %maximum_select_fusion.10, pred[]{:T(512)S(6)} %eq.14), kind=kOutput, calls=%fused_computation.60 | convolution fusion | flops 3240492288 | bytes 12061697 | tf_op jit(solution)/shard_map/dot_general | solution.py:54
  132.2 0.1 reduce_max.58
  132.3 71.0 %collective-permute-done.3 = bf16[512,2048]{1,0:T(8,128)(2,1)} collective-permute-done((bf16[512,2048]{1,0:T(8,128)(2,1)S(1)}, bf16[512,2048]{1,0:T(8,128)(2,1)}, u32[]{:S(2)}, u32[]{:S(2)}) %collective-permute-start.3) | collective-permute-done | bytes 2097184 | tf_op jit(solution)/shard_map/ppermute | solution.py:44
  203.2 8.9 %fusion.35 = (f32[768]{0:T(1024)S(1)}, f32[512,768]{1,0:T(8,128)}) fusion(bf16[768,4096]{1,0:T(8,128)(2,1)} %all-gather.2.cloned.1.call-done, bf16[512,2048]{1,0:T(8,128)(2,1)} %collective-permute-done.3, bf16[512,2048]{1,0:T(8,128)(2,1)S(1)} %maximum_select_fusion.9, pred[]{:T(512)S(6)} %eq.14), kind=kOutput, calls=%fused_computation.59 | convolution fusion | flops 3240492288 | bytes 12061697 | tf_op jit(solution)/shard_map/dot_general | solution.py:54
  212.1 0.1 reduce_max.56
  212.2 10.0 %fusion.37 = (f32[768]{0:T(1024)S(1)}, f32[512,768]{1,0:T(8,128)}) fusion(bf16[768,4096]{1,0:T(8,128)(2,1)} %all-gather.2.cloned.1.call-done, bf16[512,2048]{1,0:T(8,128)(2,1)} %collective-permute-done.7, bf16[512,2048]{1,0:T(8,128)(2,1)} %maximum_select_fusion.11, pred[]{:T(512)S(6)} %eq.14), kind=kOutput, calls=%fused_computation.61 | convolution fusion | flops 3240492288 | bytes 12061697 | tf_op jit(solution)/shard_map/dot_general | solution.py:54
  222.3 3.1 %exponential_reduce_fusion.2 = (f32[768]{0:T(1024)S(1)}, f32[768]{0:T(1024)S(1)}, f32[768]{0:T(1024)S(1)}, f32[768]{0:T(1024)S(1)}, f32[768]{0:T(1024)S(1)}, /*i...) fusion(f32[512,768]{1,0:T(8,128)} %get-tuple-element.27, f32[768]{0:T(1024)S(1)} %get-tuple-element.26, ...), kind=kLoop, calls=%fused_computation.42 | loop fusion | flops 7858176 | bytes 6339584 | tf_op jit(solution)/shard_map/reduce_sum | solution.py:21
  225.5 0.1 reduce_sum.108
  225.8 0.6 multiply_add_fusion
  226.4 6.1 %all-to-all-start.1 = ((f32[8,1,96]{2,1,0:T(1,128)}), f32[8,1,96]{2,1,0:T(1,128)S(1)}, u32[]{:S(2)}, u32[]{:S(2)}) async-start(f32[8,1,96]{2,1,0:T(1,128)} %bitcast.2), calls=%async_computation.1 | async-start | bytes 8192 | tf_op jit(solution)/shard_map/all_to_all | solution.py:68
  232.5 0.1 add.131
  232.5 6.4 %all-to-all-done.1 = f32[8,1,96]{2,1,0:T(1,128)S(1)} async-done(((f32[8,1,96]{2,1,0:T(1,128)}), f32[8,1,96]{2,1,0:T(1,128)S(1)}, u32[]{:S(2)}, u32[]{:S(2)}) %all-to-all-start.1) | async-done | bytes 3104 | tf_op jit(solution)/shard_map/all_to_all | solution.py:68
  238.9 8.8 %all_to_all.24 = f32[8,1,96]{2,1,0:T(1,128)S(1)} all-to-all(f32[8,1,96]{2,1,0:T(1,128)S(1)} %add.131), channel_id=1, replica_groups=mesh['dp'=4,'tensor'=8] {'tensor'}, dimensions={0} | all-to-all | bytes 6144 | tf_op jit(solution)/shard_map/all_to_all | solution.py:74
  247.8 3.3 %all-to-all-start = ((f32[8,1,96]{2,1,0:T(1,128)}), f32[8,1,96]{2,1,0:T(1,128)S(1)}, u32[]{:S(2)}, u32[]{:S(2)}) async-start(f32[8,1,96]{2,1,0:T(1,128)} %bitcast), calls=%async_computation | async-start | bytes 8192 | tf_op jit(solution)/shard_map/all_to_all | solution.py:71
  251.2 6.4 %all-to-all-done = f32[8,1,96]{2,1,0:T(1,128)S(1)} async-done(((f32[8,1,96]{2,1,0:T(1,128)}), f32[8,1,96]{2,1,0:T(1,128)S(1)}, u32[]{:S(2)}, u32[]{:S(2)}) %all-to-all-start) | async-done | bytes 3104 | tf_op jit(solution)/shard_map/all_to_all | solution.py:71
  257.6 1.1 fusion.32
  258.7 38.5 %psum.7 = f32[]{:T(128)} all-reduce(f32[]{:T(128)} %get-tuple-element.10), channel_id=1, replica_groups=mesh['dp'=4,'tensor'=8] {'dp','tensor'}, use_global_device_ids=true, to_apply=%region_16.17 | all-reduce | flops 1 | bytes 8 | tf_op jit(solution)/shard_map/psum | solution.py:82
  (27 shorter events, 0.5 us)
Async XLA Ops:
  7.2 105.1 %all-gather.2.cloned.1.call-start = ((), (), s32[]{:S(2)}) async-start(), calls=%async_computation.3 | async-start | bytes 7077888 | tf_op jit(solution)/shard_map/all_gather | solution.py:30
  11.8 3.1 %collective-permute-start = (bf16[512,1024]{1,0:T(8,128)(2,1)}, bf16[512,1024]{1,0:T(8,128)(2,1)}, u32[]{:S(2)}, u32[]{:S(2)}) collective-permute-start(bf16[512,1024]{1,0:T(8,128)(2,1)} %get-tuple-element.17), channel_id=1, source_target_pairs={{0,8},{8,0},{16,24},{24,16},{1,9},{9,1},{17,25},{25,17},{2,10},{10... | collective-permute-start | bytes 3145736 | tf_op jit(solution)/shard_map/ppermute | solution.py:44
  12.2 10.4 %collective-permute-start.4 = (bf16[512,1024]{1,0:T(8,128)(2,1)S(1)}, bf16[512,1024]{1,0:T(8,128)(2,1)}, u32[]{:S(2)}, u32[]{:S(2)}) collective-permute-start(bf16[512,1024]{1,0:T(8,128)(2,1)S(1)} %get-tuple-element.19), channel_id=1, source_target_pairs={{0,8},{8,0},{16,24},{24,16},{1,9},{9,1},{17,25},{25,17},{2,10},{10... | collective-permute-start | bytes 3145736 | tf_op jit(solution)/shard_map/ppermute | solution.py:44
  19.3 49.6 %collective-permute-start.1 = (bf16[512,2048]{1,0:T(8,128)(2,1)}, bf16[512,2048]{1,0:T(8,128)(2,1)}, u32[]{:S(2)}, u32[]{:S(2)}) collective-permute-start(bf16[512,2048]{1,0:T(8,128)(2,1)} %maximum_select_fusion.8), channel_id=1, source_target_pairs={{0,16},{8,24},{16,0},{24,8},{1,17},{9,25},{17,1},{25,9},{2,18},{10... | collective-permute-start | bytes 6291464 | tf_op jit(solution)/shard_map/ppermute | solution.py:44
  22.2 4.4 %collective-permute-start.6 = (bf16[512,1024]{1,0:T(8,128)(2,1)S(1)}, bf16[512,1024]{1,0:T(8,128)(2,1)}, u32[]{:S(2)}, u32[]{:S(2)}) collective-permute-start(bf16[512,1024]{1,0:T(8,128)(2,1)S(1)} %get-tuple-element.18), channel_id=1, source_target_pairs={{0,8},{8,0},{16,24},{24,16},{1,9},{9,1},{17,25},{25,17},{2,10},{10... | collective-permute-start | bytes 3145736 | tf_op jit(solution)/shard_map/ppermute | solution.py:44
  22.2 10.1 %collective-permute-start.2 = (bf16[512,1024]{1,0:T(8,128)(2,1)S(1)}, bf16[512,1024]{1,0:T(8,128)(2,1)}, u32[]{:S(2)}, u32[]{:S(2)}) collective-permute-start(bf16[512,1024]{1,0:T(8,128)(2,1)S(1)} %get-tuple-element.16), channel_id=1, source_target_pairs={{0,8},{8,0},{16,24},{24,16},{1,9},{9,1},{17,25},{25,17},{2,10},{10... | collective-permute-start | bytes 3145736 | tf_op jit(solution)/shard_map/ppermute | solution.py:44
  26.5 95.7 %collective-permute-start.5 = (bf16[512,2048]{1,0:T(8,128)(2,1)}, bf16[512,2048]{1,0:T(8,128)(2,1)}, u32[]{:S(2)}, u32[]{:S(2)}) collective-permute-start(bf16[512,2048]{1,0:T(8,128)(2,1)} %maximum_select_fusion.10), channel_id=1, source_target_pairs={{0,16},{8,24},{16,0},{24,8},{1,17},{9,25},{17,1},{25,9},{2,18},{10... | collective-permute-start | bytes 6291464 | tf_op jit(solution)/shard_map/ppermute | solution.py:44
  30.2 182.0 %collective-permute-start.7 = (bf16[512,2048]{1,0:T(8,128)(2,1)}, bf16[512,2048]{1,0:T(8,128)(2,1)}, u32[]{:S(2)}, u32[]{:S(2)}) collective-permute-start(bf16[512,2048]{1,0:T(8,128)(2,1)} %maximum_select_fusion.11), channel_id=1, source_target_pairs={{0,16},{8,24},{16,0},{24,8},{1,17},{9,25},{17,1},{25,9},{2,18},{10... | collective-permute-start | bytes 6291464 | tf_op jit(solution)/shard_map/ppermute | solution.py:44
  34.6 168.6 %collective-permute-start.3 = (bf16[512,2048]{1,0:T(8,128)(2,1)S(1)}, bf16[512,2048]{1,0:T(8,128)(2,1)}, u32[]{:S(2)}, u32[]{:S(2)}) collective-permute-start(bf16[512,2048]{1,0:T(8,128)(2,1)S(1)} %maximum_select_fusion.9), channel_id=1, source_target_pairs={{0,16},{8,24},{16,0},{24,8},{1,17},{9,25},{17,1},{25,9},{2,18},{10... | collective-permute-start | bytes 6291464 | tf_op jit(solution)/shard_map/ppermute | solution.py:44
  212.2 10.1 %copy-start = (f32[512,768]{1,0:T(8,128)S(1)}, f32[512,768]{1,0:T(8,128)}, u32[]{:S(2)}) copy-start(f32[512,768]{1,0:T(8,128)} %get-tuple-element.33) | copy-start | bytes 4718596
  212.2 10.1 %copy-start.1 = (f32[512,768]{1,0:T(8,128)S(1)}, f32[512,768]{1,0:T(8,128)}, u32[]{:S(2)}) copy-start(f32[512,768]{1,0:T(8,128)} %get-tuple-element.29) | copy-start | bytes 4718596
  212.2 10.1 %copy-start.2 = (s32[768]{0:T(1024)S(1)}, s32[768]{0:T(1024)}, u32[]{:S(2)}) copy-start(s32[768]{0:T(1024)} %param.5) | copy-start | bytes 9220
  226.4 12.6 %all-to-all-start.1 = ((f32[8,1,96]{2,1,0:T(1,128)}), f32[8,1,96]{2,1,0:T(1,128)S(1)}, u32[]{:S(2)}, u32[]{:S(2)}) async-start(f32[8,1,96]{2,1,0:T(1,128)} %bitcast.2), calls=%async_computation.1 | async-start | bytes 8192 | tf_op jit(solution)/shard_map/all_to_all | solution.py:68
  247.8 9.8 %all-to-all-start = ((f32[8,1,96]{2,1,0:T(1,128)}), f32[8,1,96]{2,1,0:T(1,128)S(1)}, u32[]{:S(2)}, u32[]{:S(2)}) async-start(f32[8,1,96]{2,1,0:T(1,128)} %bitcast), calls=%async_computation | async-start | bytes 8192 | tf_op jit(solution)/shard_map/all_to_all | solution.py:71
Sparse Core Ops, SparseCore 0:
  10.0 102.1 all-gather.1
